TPU v7x, 32 devices: a whole 2x2x4 slice. The times are simulated.
32 devices in a mesh: dp: 8 (over z, x), narrow: 4 (over y, core).
Axes of the slice: x: 2, y: 2, z: 4, core: 2. Of those that a mesh axis runs over, the one named last changes fastest.
Arguments:
- wave: float32 [1313280], P(('dp', 'narrow')), may hold values from -6 to 6
- clip_ids: int32 [4096], P(('dp', 'narrow')), may hold values from 0 to 95, never falling along the last dimension, each value on 1 to 128 neighbouring positions
- span_starts: int32 [4096], P(('dp', 'narrow')), may hold values 0 or 1
- step_count: int32 [1], replicated, may hold values from 2 to 20
- conv_small: float32 [12, 512], replicated, as said below
- conv_stack: float32 [8192, 512], P(('dp', 'narrow')), may hold values from -0.25 to 0.25
- side: float32 [768, 2192], P('dp', 'narrow'), may hold values from -0.21875 to 0.21875
- vectors: float32 [10, 768], replicated, as said below
- block: float32 [3, 768, 3072], P(None, 'dp', 'narrow')
- teacher_block: float32 [3, 768, 3072], P(None, 'dp', 'narrow')
- teacher_vectors: float32 [10, 768], replicated, as said below
- small_mean: float32 [12, 512], replicated, may hold values from -4.4428212e-05 to 4.4428212e-05
- small_square: float32 [12, 512], replicated, may hold values from 1.2336662e-10 to 4.934665e-10
- stack_mean: float32 [8192, 512], P(('dp', 'narrow')), may hold values from -1.1107053e-05 to 1.1107053e-05
- stack_square: float32 [8192, 512], P(('dp', 'narrow')), may hold values from 7.710414e-12 to 3.0841656e-11
- side_mean: float32 [768, 2192], P('dp', 'narrow'), may hold values from -1.1107053e-05 to 1.1107053e-05
- side_square: float32 [768, 2192], P('dp', 'narrow'), may hold values from 7.710414e-12 to 3.0841656e-11
- vector_mean: float32 [10, 768], replicated, may hold values from -4.4428212e-05 to 4.4428212e-05
- vector_square: float32 [10, 768], replicated, may hold values from 1.2336662e-10 to 4.934665e-10
- block_momentum: float32 [3, 768, 3072], P(None, 'dp', 'narrow'), may hold values from -1.1107053e-05 to 1.1107053e-05
Outputs:
- loss: float32 [], replicated
- grad_norm: float32 [], replicated
- conv_small_next: float32 [12, 512], replicated
- small_mean_next: float32 [12, 512], replicated
- small_square_next: float32 [12, 512], replicated
- conv_stack_next: float32 [8192, 512], P(('dp', 'narrow'))
- stack_mean_next: float32 [8192, 512], P(('dp', 'narrow'))
- stack_square_next: float32 [8192, 512], P(('dp', 'narrow'))
- side_next: float32 [768, 2192], P('dp', 'narrow')
- side_mean_next: float32 [768, 2192], P('dp', 'narrow')
- side_square_next: float32 [768, 2192], P('dp', 'narrow')
- vectors_next: float32 [10, 768], replicated
- vector_mean_next: float32 [10, 768], replicated
- vector_square_next: float32 [10, 768], replicated
- block_next: float32 [3, 768, 3072], P(None, 'dp', 'narrow')
- momentum_next: float32 [3, 768, 3072], P(None, 'dp', 'narrow')
- teacher_block_next: float32 [3, 768, 3072], P(None, 'dp', 'narrow')
- teacher_vectors_next: float32 [10, 768], replicated
- block_copy: bfloat16 [3, 768, 3072], P(None, 'dp', 'narrow')
Inputs may be any that keep to these rules, and one draw needn't show every extreme that they name: `clip_ids`: clip numbers never fall along the frames; a clip has 1 to 128 frames, and some clip has exactly 128. `conv_small`: rows 10 are positive gains. `vectors`: rows 0, 2, 4 are positive gains. `teacher_vectors`: rows 0, 2, 4 are positive gains.
All inputs are finite; a program needn't handle non-finite values. No bound on the sum of `span_starts` on one device may be relied on, other than what follows from the above.
Results may differ from a plain program's by a relative error of at most 0.0025.
The roundings to bfloat16 on the way count: a program that leaves them out, or rounds other values in their place, can miss the bound.
Values may be sent and summed in bfloat16 or wider, within the bound.
No kernel may reach another device: no remote copies, remote signals or barrier semaphores. Data moves between devices by JAX's collectives and lax.ppermute only.
A program may use at most 448 MiB of HBM per device.

v0:
```python
import math
import jax
import jax.numpy as jnp
from jax import lax
from jax.sharding import PartitionSpec as P

D = 768
HEADS = 12
HEAD_DIM = 64
CH = 512
GROUPS = 16
POS_K = 19
SPAN = 10
EPS = 1e-05
VAR_FLOOR = 0.1
CLIP_LIMIT = 0.01
LR_ADAM = 0.03
LR_MUON = 2.0
DECAY = 0.5
WEIGHT_DECAY = 0.01
EMA_RATE = 0.5
KERNELS = (3, 3, 3, 3, 2, 2)
COEFF_A = 3.4445
COEFF_B = -4.775
COEFF_C = 2.0315
HIGHEST = lax.Precision.HIGHEST


def rounded(values):
    return lax.optimization_barrier(values.astype(jnp.bfloat16)).astype(jnp.float32)


def low(values):
    return values + lax.stop_gradient(rounded(values) - values)


def low_back(values):
    return rounded(values) + lax.stop_gradient(values - rounded(values))


def bprod(left_side, right_side):
    return low_back(jnp.einsum("bmk,bkn->bmn", left_side, right_side, precision=HIGHEST))


def matmul(left_side, right_side):
    return bprod(left_side[None], right_side[None])[0]


def layer_norm(values, gain, shift):
    center = values - jnp.mean(values, axis=-1, keepdims=True)
    spread = jnp.mean(center * center, axis=-1, keepdims=True)
    return center * lax.rsqrt(spread + EPS) * gain + shift


def strided_taps(values, kernel, stride, rows_out):
    return jnp.concatenate(
        [
            lax.slice_in_dim(values, offset, offset + stride * (rows_out - 1) + 1, stride, 0)
            for offset in range(kernel)
        ],
        axis=1,
    )


def encode(conv_small, conv_stack, side, vectors, wave):
    frames = (wave.shape[0] - 80) // 320
    length = 64 * frames + 15
    hidden = strided_taps(low(wave)[:, None], 10, 5, length)
    hidden = low(jax.nn.gelu(matmul(hidden, conv_small[:10]), approximate=False))
    row_offset = 0
    for kernel in KERNELS:
        length = (length - kernel) // 2 + 1
        tap_rows = strided_taps(hidden, kernel, 2, length)
        hidden = jax.nn.gelu(
            matmul(tap_rows, conv_stack[row_offset : row_offset + kernel * CH]), approximate=False
        )
        row_offset = row_offset + kernel * CH
        if row_offset < conv_stack.shape[0]:
            hidden = low(hidden)
    normed = low(layer_norm(hidden, conv_small[10], conv_small[11]))
    return matmul(normed, side[:, :CH].T) + vectors[6]


def neighbours(segment):
    frames = segment.shape[0]
    reach = POS_K // 2
    padded = jnp.pad(segment, (reach, reach), constant_values=-1)
    return jnp.stack(
        [padded[offset : offset + frames] == segment for offset in range(POS_K)], 0
    ).astype(jnp.float32)[:, :, None]


def masked_of(starts):
    frames = starts.shape[0]
    padded = jnp.pad(starts, (SPAN - 1, 0))
    return (
        jnp.max(jnp.stack([padded[offset : offset + frames] for offset in range(SPAN)], 0), axis=0)
        > 0
    )


def position(values, side, pos_bias, nearby):
    frames = values.shape[0]
    group_width = D // GROUPS
    reach = POS_K // 2
    padded = jnp.pad(low(values), ((reach, reach), (0, 0)))
    tap_rows = jnp.stack([padded[offset : offset + frames] for offset in range(POS_K)], 0) * nearby
    tap_rows = (
        tap_rows.reshape(POS_K, frames, GROUPS, group_width)
        .transpose(2, 1, 0, 3)
        .reshape(GROUPS, frames, POS_K * group_width)
    )
    kernel = side[:, CH : CH + POS_K * group_width].reshape(GROUPS, group_width, POS_K, group_width)
    kernel = kernel.transpose(0, 2, 1, 3).reshape(GROUPS, POS_K * group_width, group_width)
    mixed = bprod(tap_rows, kernel).transpose(1, 0, 2).reshape(frames, D)
    return jax.nn.gelu(mixed + pos_bias, approximate=False)


def transform(values, side, block, vectors, nearby, attend):
    frames = values.shape[0]
    hidden = layer_norm(values + position(values, side, vectors[7], nearby), vectors[0], vectors[1])
    triple = low(matmul(low(hidden), block[0][:, : 3 * D]))
    heads = triple.reshape(frames, 3, HEADS, HEAD_DIM).transpose(1, 2, 0, 3)
    scores = bprod(heads[0], heads[1].transpose(0, 2, 1)) / math.sqrt(HEAD_DIM)
    scores = jnp.where(attend[None], scores, -1e30)
    weights = low(jax.nn.softmax(scores, axis=-1))
    mixed = bprod(weights, heads[2]).transpose(1, 0, 2).reshape(frames, D)
    hidden = layer_norm(hidden + matmul(low(mixed), block[0][:, 3 * D :]), vectors[2], vectors[3])
    inner = low(jax.nn.gelu(matmul(low(hidden), block[1]), approximate=False))
    return layer_norm(hidden + matmul(inner, block[2].T), vectors[4], vectors[5])


def target_of(feats, side, teacher_block, teacher_vectors, nearby, attend):
    output = transform(feats, side, teacher_block, teacher_vectors, nearby, attend)
    member = attend.astype(jnp.float32)
    clip_size = jnp.sum(member, axis=1, keepdims=True)
    average = jnp.dot(member, output, precision=HIGHEST) / clip_size
    center = output - average
    spread = jnp.dot(member, center * center, precision=HIGHEST) / clip_size
    return center * lax.rsqrt(jnp.maximum(spread, VAR_FLOOR))


def student_loss(feats, side, block, vectors, nearby, attend, masked, target, total):
    chosen = masked[:, None]
    values = jnp.where(chosen, vectors[9], feats)
    hidden = transform(values, side, block, vectors, nearby, attend)
    predict = matmul(low(hidden), side[:, CH + POS_K * (D // GROUPS) :]) + vectors[8]
    error = jnp.where(chosen, predict - target, 0.0)
    return jnp.sum(error * error) / (total * math.sqrt(D))


def local_step(
    wave,
    segment,
    starts,
    conv_small,
    conv_stack,
    side,
    vectors,
    block,
    teacher_block,
    teacher_vectors,
    total,
):
    nearby = neighbours(segment)
    attend = segment[:, None] == segment[None, :]
    masked = masked_of(starts)
    feats, encode_back = jax.vjp(
        lambda small_part, stack_part, side_part, vector_part: encode(
            low(small_part), low(stack_part), low(side_part), low(vector_part), wave
        ),
        conv_small,
        conv_stack,
        side,
        vectors,
    )
    target = target_of(feats, low(side), low(teacher_block), low(teacher_vectors), nearby, attend)
    loss_part, student_back = jax.vjp(
        lambda feat_part, side_part, block_part, vector_part: student_loss(
            feat_part,
            low(side_part),
            low(block_part),
            low(vector_part),
            nearby,
            attend,
            masked,
            target,
            total,
        ),
        feats,
        side,
        block,
        vectors,
    )
    feat_grad, side_two, block_grad, vector_two = student_back(jnp.ones_like(loss_part))
    small_grad, stack_grad, side_one, vector_one = encode_back(feat_grad)
    return (
        loss_part,
        small_grad,
        stack_grad,
        side_one + side_two,
        block_grad,
        vector_one + vector_two,
    )


def adamw(weight, grad, first, second, power):
    first = DECAY * first + (1.0 - DECAY) * grad
    second = DECAY * second + (1.0 - DECAY) * grad * grad
    unbias = 1.0 - power
    step_size = first / unbias / (jnp.sqrt(second / unbias) + 1e-08)
    return (weight - LR_ADAM * (step_size + WEIGHT_DECAY * weight), first, second)


def orthogonal(matrix, gram_total):
    blocks = matrix
    for iteration in range(5):
        gram_matrix = gram_total(jnp.einsum("brc,bsc->brs", blocks, blocks, precision=HIGHEST))
        if iteration == 0:
            scales = 1.0 / (jnp.sqrt(jnp.trace(gram_matrix, axis1=1, axis2=2)) + 1e-07)
            blocks = blocks * scales[:, None, None]
            gram_matrix = gram_matrix * (scales * scales)[:, None, None]
        polynom = COEFF_B * gram_matrix + COEFF_C * jnp.einsum(
            "brs,bst->brt", gram_matrix, gram_matrix, precision=HIGHEST
        )
        blocks = COEFF_A * blocks + jnp.einsum("brs,bsc->brc", polynom, blocks, precision=HIGHEST)
    return blocks.reshape(matrix.shape)


def apply_updates(factor, power, weights, grads, states, gram_total):
    (
        small_weight,
        stack_weight,
        side_weight,
        vector_weight,
        block_weight,
        teacher_weight,
        teacher_vector,
    ) = weights
    small_grad, stack_grad, side_grad, block_grad, vector_grad = grads
    small_next = adamw(small_weight, factor * small_grad, states[0], states[1], power)
    stack_next = adamw(stack_weight, factor * stack_grad, states[2], states[3], power)
    side_next = adamw(side_weight, factor * side_grad, states[4], states[5], power)
    vector_next = adamw(vector_weight, factor * vector_grad, states[6], states[7], power)
    momentum = DECAY * states[8] + factor * block_grad
    block_next = block_weight * (1.0 - LR_MUON * WEIGHT_DECAY) - LR_MUON * orthogonal(
        momentum, gram_total
    )
    teacher_next = EMA_RATE * teacher_weight + (1.0 - EMA_RATE) * block_next
    teacher_vec_next = EMA_RATE * teacher_vector + (1.0 - EMA_RATE) * vector_next[0]
    return (
        small_next
        + stack_next
        + side_next
        + vector_next
        + (block_next, momentum, teacher_next, teacher_vec_next, block_next.astype(jnp.bfloat16))
    )


def narrow_total(gram_matrix):
    return lax.psum(gram_matrix, "narrow")


def per_device(
    wave,
    clip_ids,
    span_starts,
    step_count,
    conv_small,
    conv_stack,
    side,
    vectors,
    block,
    teacher_block,
    teacher_vectors,
    small_mean,
    small_square,
    stack_mean,
    stack_square,
    side_mean,
    side_square,
    vector_mean,
    vector_square,
    block_momentum,
):
    parts = (
        block.astype(jnp.bfloat16),
        teacher_block.astype(jnp.bfloat16),
        side.astype(jnp.bfloat16),
    )
    parts = (
        lax.all_gather(parts[0], "narrow", axis=2, tiled=True),
        lax.all_gather(parts[1], "narrow", axis=2, tiled=True),
        lax.all_gather(parts[2], "narrow", axis=1, tiled=True),
    )
    parts = (
        lax.all_gather(parts[0], "dp", axis=1, tiled=True),
        lax.all_gather(parts[1], "dp", axis=1, tiled=True),
        lax.all_gather(parts[2], "dp", axis=0, tiled=True),
    )
    whole_block = parts[0].astype(jnp.float32)
    whole_teacher = parts[1].astype(jnp.float32)
    whole_side = parts[2].astype(jnp.float32)
    whole_stack = lax.all_gather(
        conv_stack.astype(jnp.bfloat16), ("dp", "narrow"), axis=0, tiled=True
    ).astype(jnp.float32)
    masked_here = jnp.sum(masked_of(span_starts).astype(jnp.float32))
    total = jnp.maximum(lax.psum(masked_here, ("dp", "narrow")), 1.0)
    loss_part, small_grad, stack_grad, side_grad, block_grad, vector_grad = local_step(
        wave,
        clip_ids,
        span_starts,
        conv_small,
        whole_stack,
        whole_side,
        vectors,
        whole_block,
        whole_teacher,
        teacher_vectors,
        total,
    )
    row_parts = [
        lax.psum_scatter(block_grad[matrix_index], "dp", scatter_dimension=0, tiled=True)
        for matrix_index in range(3)
    ]
    side_rows = lax.psum_scatter(side_grad, "dp", scatter_dimension=0, tiled=True)
    pieces = (
        lax.psum_scatter(jnp.stack(row_parts, 0), "narrow", scatter_dimension=2, tiled=True),
        lax.psum_scatter(side_rows, "narrow", scatter_dimension=1, tiled=True),
    )
    block_piece = pieces[0]
    side_piece = pieces[1]
    stack_piece = lax.psum_scatter(stack_grad, ("dp", "narrow"), scatter_dimension=0, tiled=True)
    small_total, vector_total, loss_value = lax.psum(
        (small_grad, vector_grad, loss_part), ("dp", "narrow")
    )
    shard_squares = (
        jnp.sum(block_piece * block_piece)
        + jnp.sum(side_piece * side_piece)
        + jnp.sum(stack_piece * stack_piece)
    )
    grad_norm = jnp.sqrt(
        lax.psum(shard_squares, ("dp", "narrow"))
        + jnp.sum(small_total * small_total)
        + jnp.sum(vector_total * vector_total)
    )
    factor = jnp.minimum(1.0, CLIP_LIMIT / (grad_norm + 1e-06))
    power = jnp.power(DECAY, step_count[0].astype(jnp.float32))
    updates = apply_updates(
        factor,
        power,
        (conv_small, conv_stack, side, vectors, block, teacher_block, teacher_vectors),
        (small_total, stack_piece, side_piece, block_piece, vector_total),
        (
            small_mean,
            small_square,
            stack_mean,
            stack_square,
            side_mean,
            side_square,
            vector_mean,
            vector_square,
            block_momentum,
        ),
        narrow_total,
    )
    return (
        loss_value,
        grad_norm,
        updates[0],
        updates[1],
        updates[2],
        updates[3],
        updates[4],
        updates[5],
        updates[6],
        updates[7],
        updates[8],
        updates[9],
        updates[10],
        updates[11],
        updates[12],
        updates[13],
        updates[14],
        updates[15],
        updates[16],
    )


def solution(mesh):
    in_specs = (
        P(("dp", "narrow")),
        P(("dp", "narrow")),
        P(("dp", "narrow")),
        P(),
        P(),
        P(("dp", "narrow"), None),
        P("dp", "narrow"),
        P(),
        P(None, "dp", "narrow"),
        P(None, "dp", "narrow"),
        P(),
        P(),
        P(),
        P(("dp", "narrow"), None),
        P(("dp", "narrow"), None),
        P("dp", "narrow"),
        P("dp", "narrow"),
        P(),
        P(),
        P(None, "dp", "narrow"),
    )
    out_specs = (
        P(),
        P(),
        P(),
        P(),
        P(),
        P(("dp", "narrow"), None),
        P(("dp", "narrow"), None),
        P(("dp", "narrow"), None),
        P("dp", "narrow"),
        P("dp", "narrow"),
        P("dp", "narrow"),
        P(),
        P(),
        P(),
        P(None, "dp", "narrow"),
        P(None, "dp", "narrow"),
        P(None, "dp", "narrow"),
        P(),
        P(None, "dp", "narrow"),
    )
    return jax.shard_map(
        per_device, mesh=mesh, in_specs=in_specs, out_specs=out_specs, check_vma=False
    )
```

profile of v0, /device:TPU:0, one launch (start us, length us, event | category | flops | bytes accessed | tf_op | source)
XLA Modules:
  0.0 2137.3 jit_solution(9828727559107884883)
XLA Ops:
  34.9 39.8 %psum.70 = f32[]{:T(128)} all-reduce(f32[]{:T(128)} %get-tuple-element.160), channel_id=1, replica_groups=mesh['dp'=8,'narrow'=4] {'dp','narrow'}, use_global_device_ids=true, to_apply=%region_21.22 | all-reduce | flops 1 | bytes 8 | tf_op jit(solution)/shard_map/psum | solution.py:308
  115.7 39.3 %fusion.62 = (bf16[8207,512]{1,0:T(8,128)(2,1)}, f32[8207,512]{1,0:T(8,128)}) fusion(f32[8207,512]{1,0:T(8,128)S(1)} %fusion.404, bf16[1,8207,512]{2,1,0:T(8,128)(2,1)S(1)} %convert_bitcast_fusion), kind=kLoop, calls=%fused_computation.104 | loop fusion | flops 285734912 | bytes 50423808 | tf_op jit(solution)/shard_map/jvp()/convert_element_type | solution.py:30
  172.4 41.3 %slice.450 = f32[4103,512]{1,0:T(8,128)} slice(f32[8207,512]{1,0:T(8,128)} %subtract_add_fusion.2), slice={[0:8205:2], [0:512:1]} | slice | bytes 16805888 | tf_op jit(solution)/shard_map/jvp()/slice | solution.py:58
  213.7 41.2 %slice.451 = f32[4103,512]{1,0:T(8,128)} slice(f32[8207,512]{1,0:T(8,128)} %subtract_add_fusion.2), slice={[1:8206:2], [0:512:1]} | slice | bytes 16805888 | tf_op jit(solution)/shard_map/jvp()/slice | solution.py:58
  254.9 41.7 %slice.452 = f32[4103,512]{1,0:T(8,128)} slice(f32[8207,512]{1,0:T(8,128)} %subtract_add_fusion.2), slice={[2:8207:2], [0:512:1]} | slice | bytes 16805888 | tf_op jit(solution)/shard_map/jvp()/slice | solution.py:58
  351.8 45.2 %fusion.4 = f32[4103,512]{1,0:T(8,128)S(1)} fusion(f32[4103,512]{1,0:T(8,128)} %slice.452, f32[4103,512]{1,0:T(8,128)} %slice.451, f32[4103,512]{1,0:T(8,128)} %slice.450, f32[8192,512]{1,0:T(8,128)} %subtract_add_fusion.4), kind=kOutput, calls=%fused_computation.11 | convolution fusion | flops 38733369344 | bytes 36763648 | tf_op jit(solution)/shard_map/jvp(bmk,bkn->bmn)/dot_general | solution.py:42
  397.6 20.1 fusion.95
  427.5 21.1 slice.454
  448.6 21.0 slice.455
  469.7 21.5 %slice.456 = f32[2051,512]{1,0:T(8,128)} slice(f32[4103,512]{1,0:T(8,128)} %subtract_add_fusion.5), slice={[2:4103:2], [0:512:1]} | slice | bytes 8400896 | tf_op jit(solution)/shard_map/jvp()/slice | solution.py:58
  491.2 24.3 %fusion.28 = f32[2051,512]{1,0:T(8,128)S(1)} fusion(f32[2051,512]{1,0:T(8,128)} %slice.456, f32[2051,512]{1,0:T(8,128)} %slice.455, f32[2051,512]{1,0:T(8,128)} %slice.454, f32[8192,512]{1,0:T(8,128)} %subtract_add_fusion.4), kind=kOutput, calls=%fused_computation.59 | convolution fusion | flops 19361964032 | bytes 19978240 | tf_op jit(solution)/shard_map/jvp(bmk,bkn->bmn)/dot_general | solution.py:42
  767.5 22.5 %subtract_add_fusion = f32[3,768,3072]{2,1,0:T(8,128)} fusion(bf16[3,768,3072]{2,1,0:T(8,128)(2,1)} %all-gather.18.cloned.1.call-done), kind=kLoop, calls=%fused_computation.2 | loop fusion | flops 28311552 | bytes 42467328 | tf_op jit(solution)/shard_map/add | solution.py:34
  836.9 22.6 %subtract_add_fusion.1 = f32[3,768,3072]{2,1,0:T(8,128)} fusion(bf16[3,768,3072]{2,1,0:T(8,128)(2,1)} %all-gather.14.cloned.1.call-done), kind=kLoop, calls=%fused_computation.3 | loop fusion | flops 28311552 | bytes 42467328 | tf_op jit(solution)/shard_map/jvp()/add | solution.py:34
  962.6 21.4 %pad_add_fusion = f32[3,768,3072]{2,1,0:T(8,128)} fusion(f32[1,768,3072]{2,1,0:T(8,128)} %pad_bitcast_fusion, f32[1,768,3072]{2,1,0:T(8,128)} %pad_bitcast_fusion.1, f32[1,768,3072]{2,1,0:T(8,128)} %convolution_bitcast_fusion.1, f32[1,768,3072]{2,1,0:T(8,128)S(1)} %convolution_bitcast_fusion.2), kind=kLoop, calls=%fused_computation.4 | loop fusion | flops 21233664 | bytes 66060288 | tf_op jit(solution)/shard_map/transpose(jvp())/add_any | solution.py:122
  1096.6 22.2 %pad.260 = f32[512,512]{0,1:T(8,128)} pad(f32[256,512]{0,1:T(8,128)} %get-tuple-element.231, f32[]{:T(128)} %constant.65.clone.1), padding=1_0_1x0_0_0 | pad | bytes 1572868 | tf_op jit(solution)/shard_map/transpose(jvp())/pad | solution.py:58
  1118.8 20.0 pad.261
  1266.7 32.8 %pad.271 = f32[4103,512]{1,0:T(8,128)} pad(f32[2051,512]{1,0:T(8,128)} %get-tuple-element.204, f32[]{:T(128)} %constant.65.clone.1), padding=2_0_1x0_0_0 | pad | bytes 12603396 | tf_op jit(solution)/shard_map/transpose(jvp())/pad | solution.py:58
  1299.5 32.6 %pad.272 = f32[4103,512]{1,0:T(8,128)} pad(f32[2051,512]{1,0:T(8,128)} %get-tuple-element.202, f32[]{:T(128)} %constant.65.clone.1), padding=1_1_1x0_0_0 | pad | bytes 12603396 | tf_op jit(solution)/shard_map/transpose(jvp())/pad | solution.py:58
  1332.1 32.6 %pad.273 = f32[4103,512]{1,0:T(8,128)} pad(f32[2051,512]{1,0:T(8,128)} %get-tuple-element.203, f32[]{:T(128)} %constant.65.clone.1), padding=0_2_1x0_0_0 | pad | bytes 12603396 | tf_op jit(solution)/shard_map/transpose(jvp())/pad | solution.py:58
  1364.7 135.9 %reduce-scatter.15.cloned.1.call-done = f32[96,3072]{1,0:T(8,128)} async-done(((f32[768,3072]{1,0:T(8,128)}), f32[96,3072]{1,0:T(8,128)}) %reduce-scatter.15.cloned.1.call-update) | async-done | bytes 1179664 | tf_op jit(solution)/shard_map/reduce_scatter | solution.py:323
  1557.0 26.4 %fusion.91 = f32[1536,512]{1,0:T(8,128)} fusion(f32[4103,512]{1,0:T(8,128)} %slice.452, f32[4103,512]{1,0:T(8,128)S(1)} %bitcast.1359, f32[4103,512]{1,0:T(8,128)S(1)} %bitcast.1357, bf16[1,4103,512]{2,1,0:T(8,128)(2,1)S(1)} %bitcast.1368), kind=kOutput, calls=%fused_computation.150 | convolution fusion | flops 38733369344 | bytes 32556032 | tf_op jit(solution)/shard_map/transpose(jvp(bmk,bkn->bmn))/dot_general | solution.py:42
  1596.8 25.8 %fusion.85 = f32[4103,1536]{1,0:T(8,128)} fusion(bf16[1,4103,512]{2,1,0:T(8,128)(2,1)} %fusion.88, f32[8192,512]{1,0:T(8,128)} %subtract_add_fusion.4), kind=kOutput, calls=%fused_computation.141 | convolution fusion | flops 38720765952 | bytes 32557056 | tf_op jit(solution)/shard_map/transpose(jvp(bmk,bkn->bmn))/dot_general | solution.py:42
  1640.4 65.6 %pad.277 = f32[8207,512]{1,0:T(8,128)} pad(f32[4103,512]{1,0:T(8,128)} %get-tuple-element.201, f32[]{:T(128)} %constant.65.clone.1), padding=2_0_1x0_0_0 | pad | bytes 25210884 | tf_op jit(solution)/shard_map/transpose(jvp())/pad | solution.py:58
  1706.0 64.6 %pad.278 = f32[8207,512]{1,0:T(8,128)} pad(f32[4103,512]{1,0:T(8,128)} %get-tuple-element.199, f32[]{:T(128)} %constant.65.clone.1), padding=1_1_1x0_0_0 | pad | bytes 25210884 | tf_op jit(solution)/shard_map/transpose(jvp())/pad | solution.py:58
  1770.6 64.4 %pad.279 = f32[8207,512]{1,0:T(8,128)} pad(f32[4103,512]{1,0:T(8,128)} %get-tuple-element.200, f32[]{:T(128)} %constant.65.clone.1), padding=0_2_1x0_0_0 | pad | bytes 25210884 | tf_op jit(solution)/shard_map/transpose(jvp())/pad | solution.py:58
  1835.0 34.4 %fusion.55 = bf16[1,8207,512]{2,1,0:T(8,128)(2,1)} fusion(f32[8207,512]{1,0:T(8,128)} %get-tuple-element.195, f32[8207,512]{1,0:T(8,128)} %pad.279, f32[8207,512]{1,0:T(8,128)} %pad.277, f32[8207,512]{1,0:T(8,128)} %pad.278, f32[8207,512]{1,0:T(8,128)} %copy-done, bf16[1,8207,512]{2,1,0:T(8,128)(2,1)} %copy-done.2), kind=kLoop, calls=%fused_computation.94 | loop fusion | flops 79837696 | bytes 100847616 | tf_op jit(solution)/shard_map/transpose(jvp())/convert_element_type | solution.py:30
  1901.4 43.9 %all-reduce.72 = (f32[]{:T(128)}, f32[]{:T(128)}, f32[12,512]{1,0:T(8,128)S(1)}, f32[10,768]{1,0:T(8,128)S(1)}) all-reduce(f32[]{:T(128)S(6)} %div.229, f32[]{:T(128)S(6)} %add.761, f32[12,512]{1,0:T(8,128)S(1)} %pad_add_fusion.9, f32[10,768]{1,0:T(8,128)S(1)} %add_add_fusion.5), channel_id=1, replica_groups=mesh['dp'=8,'narrow'=4] {'dp','narrow'}, use_global_device_ids=true, to_apply=%region_22.23 | all-reduce | flops 13826 | bytes 110608 | tf_op jit(solution)/shard_map/psum | solution.py:334
  1956.4 26.0 %all-reduce.79.cloned.1.call-done = f32[3,96,96]{2,1,0:T(8,128)} async-done(((f32[3,96,96]{2,1,0:T(8,128)}), f32[3,96,96]{2,1,0:T(8,128)}) %all-reduce.79.cloned.1.call-update) | async-done | bytes 110608 | tf_op jit(solution)/shard_map/psum | solution.py:261
  1990.1 29.0 %all-reduce.81.cloned.1.call-done = f32[3,96,96]{2,1,0:T(8,128)} async-done(((f32[3,96,96]{2,1,0:T(8,128)}), f32[3,96,96]{2,1,0:T(8,128)}) %all-reduce.81.cloned.1.call-update) | async-done | bytes 110608 | tf_op jit(solution)/shard_map/psum | solution.py:261
  2024.0 30.5 %all-reduce.83.cloned.1.call-done = f32[3,96,96]{2,1,0:T(8,128)} async-done(((f32[3,96,96]{2,1,0:T(8,128)}), f32[3,96,96]{2,1,0:T(8,128)}) %all-reduce.83.cloned.1.call-update) | async-done | bytes 110608 | tf_op jit(solution)/shard_map/psum | solution.py:261
  2060.1 30.0 %all-reduce.85.cloned.1.call-done = f32[3,96,96]{2,1,0:T(8,128)} async-done(((f32[3,96,96]{2,1,0:T(8,128)}), f32[3,96,96]{2,1,0:T(8,128)}) %all-reduce.85.cloned.1.call-update) | async-done | bytes 110608 | tf_op jit(solution)/shard_map/psum | solution.py:261
  2100.8 24.8 %all-reduce.87.cloned.1.call-done = f32[3,96,96]{2,1,0:T(8,128)} async-done(((f32[3,96,96]{2,1,0:T(8,128)}), f32[3,96,96]{2,1,0:T(8,128)}) %all-reduce.87.cloned.1.call-update) | async-done | bytes 110608 | tf_op jit(solution)/shard_map/psum | solution.py:261
  (937 shorter events, 945.8 us)
Async XLA Ops:
  7.2 26.5 %all-gather.16.cloned.1.call-start = ((), (), s32[]{:S(2)}) async-start(), calls=%async_computation.10 | async-start | bytes 2211840 | tf_op jit(solution)/shard_map/all_gather | solution.py:293
  9.3 65.5 %copy-start.135 = (f32[41040]{0:T(1024)S(1)}, f32[41040]{0:T(1024)}, u32[]{:S(2)}) copy-start(f32[41040]{0:T(1024)} %param.20) | copy-start | bytes 492484
  9.3 292.0 %all-gather.12.cloned.1.call-start = ((), (), s32[]{:S(2)}) async-start(), calls=%async_computation.8 | async-start | bytes 2211840 | tf_op jit(solution)/shard_map/all_gather | solution.py:292
  11.4 86.8 %copy-start.140 = (f32[12,512]{1,0:T(8,128)S(1)}, f32[12,512]{1,0:T(8,128)}, u32[]{:S(2)}) copy-start(f32[12,512]{1,0:T(8,128)} %param.24) | copy-start | bytes 73732
  11.4 290.0 %all-gather.10.cloned.1.call-start = ((), (), s32[]{:S(2)}) async-start(), calls=%async_computation.7 | async-start | bytes 3981312 | tf_op jit(solution)/shard_map/all_gather | solution.py:299
  22.3 314.9 %all-gather.8.cloned.1.call-start = ((), (), s32[]{:S(2)}) async-start(), calls=%async_computation.6 | async-start | bytes 8650752 | tf_op jit(solution)/shard_map/all_gather | solution.py:304
  23.1 744.4 %all-gather.18.cloned.1.call-start = ((), (), s32[]{:S(2)}) async-start(), calls=%async_computation.11 | async-start | bytes 15925248 | tf_op jit(solution)/shard_map/all_gather | solution.py:298
  33.7 803.2 %all-gather.14.cloned.1.call-start = ((), (), s32[]{:S(2)}) async-start(), calls=%async_computation.9 | async-start | bytes 15925248 | tf_op jit(solution)/shard_map/all_gather | solution.py:297
  254.9 42.6 %copy-start.137 = (f32[10,768]{1,0:T(8,128)S(1)}, f32[10,768]{1,0:T(8,128)}, u32[]{:S(2)}) copy-start(f32[10,768]{1,0:T(8,128)} %param.30) | copy-start | bytes 92164
  301.4 1063.4 %reduce-scatter.11.cloned.1.call-start = ((), (), s32[]{:S(2)}) async-start(), calls=%async_computation.12 | async-start | bytes 10616832 | tf_op jit(solution)/shard_map/reduce_scatter | solution.py:323
  659.2 42.9 %copy-start.32 = (f32[128,768]{1,0:T(8,128)}, f32[128,768]{1,0:T(8,128)S(1)}, u32[]{:S(2)}) copy-start(f32[128,768]{1,0:T(8,128)S(1)} %get-tuple-element.175) | copy-start | bytes 1179652
  767.1 96.8 %copy-start.179 = (f32[128]{0:T(128)}, f32[128]{0:T(128)S(1)}, u32[]{:S(2)}) copy-start(f32[128]{0:T(128)S(1)} %broadcast_multiply_fusion.6) | copy-start | bytes 1540
  767.3 96.6 %copy-start.190 = (f32[128]{0:T(128)}, f32[128]{0:T(128)S(1)}, u32[]{:S(2)}) copy-start(f32[128]{0:T(128)S(1)} %fusion.431) | copy-start | bytes 1540
  767.5 96.5 %copy-start.90 = (bf16[128,768]{1,0:T(8,128)(2,1)}, bf16[128,768]{1,0:T(8,128)(2,1)S(1)}, u32[]{:S(2)}) copy-start(bf16[128,768]{1,0:T(8,128)(2,1)S(1)} %fusion.441) | copy-start | bytes 589828
  1003.8 360.9 %reduce-scatter.13.cloned.1.call-start = ((), (), s32[]{:S(2)}) async-start(), calls=%async_computation.13 | async-start | bytes 10616832 | tf_op jit(solution)/shard_map/reduce_scatter | solution.py:323
  1004.6 496.0 %reduce-scatter.15.cloned.1.call-start = ((), (), s32[]{:S(2)}) async-start(), calls=%async_computation.14 | async-start | bytes 10616832 | tf_op jit(solution)/shard_map/reduce_scatter | solution.py:323
  1005.3 870.0 %reduce-scatter.21.cloned.1.call-start = ((), (), s32[]{:S(2)}) async-start(), calls=%async_computation.22 | async-start | bytes 7962624
  1084.6 811.0 %reduce-scatter.17.cloned.1.call-start = ((), (), s32[]{:S(2)}) async-start(), calls=%async_computation.15 | async-start | bytes 4423680 | tf_op jit(solution)/shard_map/reduce_scatter | solution.py:328
  1092.9 45.9 %copy-start.19 = (f32[512,512]{0,1:T(8,128)S(1)}, f32[512,512]{0,1:T(8,128)}, u32[]{:S(2)}) copy-start(f32[512,512]{0,1:T(8,128)} %copy-done.18) | copy-start | bytes 3145732
  1092.9 45.9 %copy-start.36 = (f32[512,512]{0,1:T(8,128)S(1)}, f32[512,512]{0,1:T(8,128)}, u32[]{:S(2)}) copy-start(f32[512,512]{0,1:T(8,128)} %copy-done.35) | copy-start | bytes 3145732
  1092.9 45.9 %copy-start.44 = (bf16[1,512,512]{1,2,0:T(8,128)(2,1)S(1)}, bf16[1,512,512]{1,2,0:T(8,128)(2,1)}, u32[]{:S(2)}) copy-start(bf16[1,512,512]{1,2,0:T(8,128)(2,1)} %copy-done.43) | copy-start | bytes 1572868
  1504.8 394.2 %reduce-scatter.19.cloned.1.call-start = ((), (), s32[]{:S(2)}) async-start(), calls=%async_computation.16 | async-start | bytes 17301504 | tf_op jit(solution)/shard_map/reduce_scatter | solution.py:333
  1594.1 388.3 %all-reduce.79.cloned.1.call-start = ((), (), s32[]{:S(2)}) async-start(), calls=%async_computation.17 | async-start | bytes 294912 | tf_op jit(solution)/shard_map/psum | solution.py:261
  1875.3 73.3 %copy-start.130 = (f32[3,96,768]{2,1,0:T(8,128)S(1)}, f32[3,96,768]{2,1,0:T(8,128)}, u32[]{:S(2)}) copy-start(f32[3,96,768]{2,1,0:T(8,128)} %param.39) | copy-start | bytes 2654212
  1877.0 74.9 %copy-start.129 = (f32[96,548]{1,0:T(8,128)S(1)}, f32[96,548]{1,0:T(8,128)}, u32[]{:S(2)}) copy-start(f32[96,548]{1,0:T(8,128)} %param.26) | copy-start | bytes 631300
  1892.1 2.2 collective-permute-start
  1951.6 67.6 %all-reduce.81.cloned.1.call-start = ((), (), s32[]{:S(2)}) async-start(), calls=%async_computation.18 | async-start | bytes 294912 | tf_op jit(solution)/shard_map/psum | solution.py:261
  1987.4 67.2 %all-reduce.83.cloned.1.call-start = ((), (), s32[]{:S(2)}) async-start(), calls=%async_computation.19 | async-start | bytes 294912 | tf_op jit(solution)/shard_map/psum | solution.py:261
  2022.9 67.2 %all-reduce.85.cloned.1.call-start = ((), (), s32[]{:S(2)}) async-start(), calls=%async_computation.20 | async-start | bytes 294912 | tf_op jit(solution)/shard_map/psum | solution.py:261
  2056.8 70.1 %copy-start.66 = (f32[3,96,768]{2,1,0:T(8,128)S(1)}, f32[3,96,768]{2,1,0:T(8,128)}, u32[]{:S(2)}) copy-start(f32[3,96,768]{2,1,0:T(8,128)} %param.29) | copy-start | bytes 2654212
  2056.8 70.1 %copy-start.67 = (f32[3,96,768]{2,1,0:T(8,128)S(1)}, f32[3,96,768]{2,1,0:T(8,128)}, u32[]{:S(2)}) copy-start(f32[3,96,768]{2,1,0:T(8,128)} %param.28) | copy-start | bytes 2654212
  2058.4 67.1 %all-reduce.87.cloned.1.call-start = ((), (), s32[]{:S(2)}) async-start(), calls=%async_computation.21 | async-start | bytes 294912 | tf_op jit(solution)/shard_map/psum | solution.py:261
  (237 other events, 2217.6 us)
Sparse Core Ops, SparseCore 0:
  10.2 23.4 all-gather.15
  35.8 20.9 all-gather.11
  59.5 65.1 all-gather.9
  128.0 76.0 all-gather.7
  206.2 194.1 all-gather.17
  402.4 193.7 all-gather.13
  1003.9 164.3 reduce-scatter.10
  1171.9 162.3 reduce-scatter.12
  1338.0 162.5 reduce-scatter.14
  1504.1 128.1 reduce-scatter.20
  1635.0 39.4 reduce-scatter.16
  1676.7 182.9 reduce-scatter.18
  1951.7 30.6 all-reduce.78
  1987.5 31.5 all-reduce.80
  2023.0 31.5 all-reduce.82
  2058.5 31.5 all-reduce.84
  2094.0 31.5 all-reduce.86
where the time goes:
time: 2160 us; the launch traced here: 2140 us
  local copies, waits for them, and re-layouts  972 us (45%)
  matrix products  397 us (18%)
  other arithmetic  342 us (16%)
  waiting for transfers between devices  289 us (13%)
  blocking collectives  107 us (5%)
  between operations  27.1 us (1%)
    pad x16, local copies, waits for them, and re-layouts, strided_taps(): lax.slice_in_dim(values, offset, offset + stride * (rows_out - 1) + 1, st...  404 us
    dot_general x54, matrix products, bprod(): jnp.einsum('bmk,bkn->bmn', left_side, right_side, precision=HIGHEST)  376 us
    slice x26, local copies, waits for them, and re-layouts, strided_taps(): lax.slice_in_dim(values, offset, offset + stride * (rows_out - 1) + 1, st...  293 us
    psum x5, waiting for transfers between devices, narrow_total(): return lax.psum(gram_matrix, 'narrow')  140 us
    reduce_scatter x3, waiting for transfers between devices, per_device(): lax.psum_scatter(block_grad[matrix_index], 'dp', scatter_dimension=0, til...  136 us
    add x18, other arithmetic, low(): return values + lax.stop_gradient(rounded(values) - values)  94 us
    convert_element_type x43, other arithmetic, rounded(): values.astype(jnp.bfloat16)  91.3 us
    convert_element_type x13, other arithmetic, rounded(): lax.optimization_barrier(values.astype(jnp.bfloat16)).astype(jnp.float32)  72.3 us
  transfers between devices with their start and end apart: 18, of which 8 were waited for; matrix products, arithmetic and copies ran while one was open for 71% of the time, Pallas kernels for 0%

commit v1 on v0

--- a/solution.py
+++ b/solution.py
@@ -258,7 +258,7 @@
 
 
 def narrow_total(gram_matrix):
-    return lax.psum(gram_matrix, "narrow")
+    return jnp.sum(lax.all_gather(gram_matrix, axis_name="narrow"), axis=0)
 
 
 def per_device(

time: 2160 us -> 2050 us (0.949)
  waiting for transfers between devices: 289 us -> 148 us
  blocking collectives: 107 us -> 148 us
    psum x5 -> x0, waiting for transfers between devices: 140 us -> none  [narrow_total(): return lax.psum(gram_matrix, 'narrow')]
    all_gather x0 -> x5, blocking collectives: none -> 40 us  [narrow_total(): return jnp.sum(lax.all_gather(gram_matrix, axis_name='narrow'), axis=0)]
    unnamed x548 -> x556, local copies, waits for them, and re-layouts: 58.9 us -> 55.1 us
  transfers between devices with their start and end apart: 18 -> 13, of which waited for: 8 -> 3; matrix products, arithmetic and copies ran while one was open for 71% -> 74% of each run, Pallas kernels for 0% -> 0%
where the time goes in v1:
time: 2050 us; the launch traced here: 2020 us
  local copies, waits for them, and re-layouts  968 us (47%)
  matrix products  389 us (19%)
  other arithmetic  342 us (17%)
  waiting for transfers between devices  148 us (7%)
  blocking collectives  148 us (7%)
  between operations  27.4 us (1%)
    pad x16, local copies, waits for them, and re-layouts, strided_taps(): lax.slice_in_dim(values, offset, offset + stride * (rows_out - 1) + 1, st...  403 us
    dot_general x54, matrix products, bprod(): jnp.einsum('bmk,bkn->bmn', left_side, right_side, precision=HIGHEST)  376 us
    slice x26, local copies, waits for them, and re-layouts, strided_taps(): lax.slice_in_dim(values, offset, offset + stride * (rows_out - 1) + 1, st...  293 us
    reduce_scatter x3, waiting for transfers between devices, per_device(): lax.psum_scatter(block_grad[matrix_index], 'dp', scatter_dimension=0, til...  136 us
    add x18, other arithmetic, low(): return values + lax.stop_gradient(rounded(values) - values)  94 us
    convert_element_type x43, other arithmetic, rounded(): values.astype(jnp.bfloat16)  91.3 us
    convert_element_type x13, other arithmetic, rounded(): lax.optimization_barrier(values.astype(jnp.bfloat16)).astype(jnp.float32)  72.2 us
    slice x38, local copies, waits for them, and re-layouts, position(): padded[offset:offset + frames]  65.7 us
  transfers between devices with their start and end apart: 13, of which 3 were waited for; matrix products, arithmetic and copies ran while one was open for 74% of the time, Pallas kernels for 0%

profile of v1, /device:TPU:0, one launch (start us, length us, event | category | flops | bytes accessed | tf_op | source)
XLA Modules:
  0.0 2024.1 jit_solution(12906304272802182615)
XLA Ops:
  34.9 39.8 %psum.35 = f32[]{:T(128)} all-reduce(f32[]{:T(128)} %get-tuple-element.160), channel_id=1, replica_groups=mesh['dp'=8,'narrow'=4] {'dp','narrow'}, use_global_device_ids=true, to_apply=%region_21.22 | all-reduce | flops 1 | bytes 8 | tf_op jit(solution)/shard_map/psum | solution.py:308
  115.7 39.3 %fusion.62 = (bf16[8207,512]{1,0:T(8,128)(2,1)}, f32[8207,512]{1,0:T(8,128)}) fusion(f32[8207,512]{1,0:T(8,128)S(1)} %fusion.404, bf16[1,8207,512]{2,1,0:T(8,128)(2,1)S(1)} %convert_bitcast_fusion), kind=kLoop, calls=%fused_computation.104 | loop fusion | flops 285734912 | bytes 50423808 | tf_op jit(solution)/shard_map/jvp()/convert_element_type | solution.py:30
  172.5 41.3 %slice.450 = f32[4103,512]{1,0:T(8,128)} slice(f32[8207,512]{1,0:T(8,128)} %subtract_add_fusion.2), slice={[0:8205:2], [0:512:1]} | slice | bytes 16805888 | tf_op jit(solution)/shard_map/jvp()/slice | solution.py:58
  213.8 41.1 %slice.451 = f32[4103,512]{1,0:T(8,128)} slice(f32[8207,512]{1,0:T(8,128)} %subtract_add_fusion.2), slice={[1:8206:2], [0:512:1]} | slice | bytes 16805888 | tf_op jit(solution)/shard_map/jvp()/slice | solution.py:58
  254.9 41.8 %slice.452 = f32[4103,512]{1,0:T(8,128)} slice(f32[8207,512]{1,0:T(8,128)} %subtract_add_fusion.2), slice={[2:8207:2], [0:512:1]} | slice | bytes 16805888 | tf_op jit(solution)/shard_map/jvp()/slice | solution.py:58
  351.9 45.2 %fusion.4 = f32[4103,512]{1,0:T(8,128)S(1)} fusion(f32[4103,512]{1,0:T(8,128)} %slice.452, f32[4103,512]{1,0:T(8,128)} %slice.451, f32[4103,512]{1,0:T(8,128)} %slice.450, f32[8192,512]{1,0:T(8,128)} %subtract_add_fusion.4), kind=kOutput, calls=%fused_computation.11 | convolution fusion | flops 38733369344 | bytes 36763648 | tf_op jit(solution)/shard_map/jvp(bmk,bkn->bmn)/dot_general | solution.py:42
  397.7 20.1 fusion.95
  427.7 21.0 %slice.454 = f32[2051,512]{1,0:T(8,128)} slice(f32[4103,512]{1,0:T(8,128)} %subtract_add_fusion.5), slice={[0:4101:2], [0:512:1]} | slice | bytes 8400896 | tf_op jit(solution)/shard_map/jvp()/slice | solution.py:58
  448.7 21.0 %slice.455 = f32[2051,512]{1,0:T(8,128)} slice(f32[4103,512]{1,0:T(8,128)} %subtract_add_fusion.5), slice={[1:4102:2], [0:512:1]} | slice | bytes 8400896 | tf_op jit(solution)/shard_map/jvp()/slice | solution.py:58
  469.7 21.5 %slice.456 = f32[2051,512]{1,0:T(8,128)} slice(f32[4103,512]{1,0:T(8,128)} %subtract_add_fusion.5), slice={[2:4103:2], [0:512:1]} | slice | bytes 8400896 | tf_op jit(solution)/shard_map/jvp()/slice | solution.py:58
  491.2 24.3 %fusion.28 = f32[2051,512]{1,0:T(8,128)S(1)} fusion(f32[2051,512]{1,0:T(8,128)} %slice.456, f32[2051,512]{1,0:T(8,128)} %slice.455, f32[2051,512]{1,0:T(8,128)} %slice.454, f32[8192,512]{1,0:T(8,128)} %subtract_add_fusion.4), kind=kOutput, calls=%fused_computation.59 | convolution fusion | flops 19361964032 | bytes 19978240 | tf_op jit(solution)/shard_map/jvp(bmk,bkn->bmn)/dot_general | solution.py:42
  604.3 19.5 slice.466
  623.8 19.9 slice.467
  767.6 22.5 %subtract_add_fusion = f32[3,768,3072]{2,1,0:T(8,128)} fusion(bf16[3,768,3072]{2,1,0:T(8,128)(2,1)} %all-gather.23.cloned.1.call-done), kind=kLoop, calls=%fused_computation.2 | loop fusion | flops 28311552 | bytes 42467328 | tf_op jit(solution)/shard_map/add | solution.py:34
  837.0 22.6 %subtract_add_fusion.1 = f32[3,768,3072]{2,1,0:T(8,128)} fusion(bf16[3,768,3072]{2,1,0:T(8,128)(2,1)} %all-gather.19.cloned.1.call-done), kind=kLoop, calls=%fused_computation.3 | loop fusion | flops 28311552 | bytes 42467328 | tf_op jit(solution)/shard_map/jvp()/add | solution.py:34
  962.8 21.4 %pad_add_fusion = f32[3,768,3072]{2,1,0:T(8,128)} fusion(f32[1,768,3072]{2,1,0:T(8,128)} %pad_bitcast_fusion, f32[1,768,3072]{2,1,0:T(8,128)} %pad_bitcast_fusion.1, f32[1,768,3072]{2,1,0:T(8,128)} %convolution_bitcast_fusion.1, f32[1,768,3072]{2,1,0:T(8,128)S(1)} %convolution_bitcast_fusion.2), kind=kLoop, calls=%fused_computation.4 | loop fusion | flops 21233664 | bytes 66060288 | tf_op jit(solution)/shard_map/transpose(jvp())/add_any | solution.py:122
  984.2 19.8 slice_bitcast_fusion.2
  1096.8 22.2 %pad.260 = f32[512,512]{0,1:T(8,128)} pad(f32[256,512]{0,1:T(8,128)} %get-tuple-element.231, f32[]{:T(128)} %constant.65.clone.1), padding=1_0_1x0_0_0 | pad | bytes 1572868 | tf_op jit(solution)/shard_map/transpose(jvp())/pad | solution.py:58
  1118.9 20.0 pad.261
  1266.9 32.8 %pad.271 = f32[4103,512]{1,0:T(8,128)} pad(f32[2051,512]{1,0:T(8,128)} %get-tuple-element.204, f32[]{:T(128)} %constant.65.clone.1), padding=2_0_1x0_0_0 | pad | bytes 12603396 | tf_op jit(solution)/shard_map/transpose(jvp())/pad | solution.py:58
  1299.7 32.6 %pad.272 = f32[4103,512]{1,0:T(8,128)} pad(f32[2051,512]{1,0:T(8,128)} %get-tuple-element.202, f32[]{:T(128)} %constant.65.clone.1), padding=1_1_1x0_0_0 | pad | bytes 12603396 | tf_op jit(solution)/shard_map/transpose(jvp())/pad | solution.py:58
  1332.2 32.5 %pad.273 = f32[4103,512]{1,0:T(8,128)} pad(f32[2051,512]{1,0:T(8,128)} %get-tuple-element.203, f32[]{:T(128)} %constant.65.clone.1), padding=0_2_1x0_0_0 | pad | bytes 12603396 | tf_op jit(solution)/shard_map/transpose(jvp())/pad | solution.py:58
  1364.7 136.0 %reduce-scatter.15.cloned.1.call-done = f32[96,3072]{1,0:T(8,128)} async-done(((f32[768,3072]{1,0:T(8,128)}), f32[96,3072]{1,0:T(8,128)}) %reduce-scatter.15.cloned.1.call-update) | async-done | bytes 1179664 | tf_op jit(solution)/shard_map/reduce_scatter | solution.py:323
  1504.9 19.7 fusion.88
  1557.1 26.4 %fusion.91 = f32[1536,512]{1,0:T(8,128)} fusion(f32[4103,512]{1,0:T(8,128)} %slice.452, f32[4103,512]{1,0:T(8,128)S(1)} %bitcast.1364, f32[4103,512]{1,0:T(8,128)S(1)} %bitcast.1362, bf16[1,4103,512]{2,1,0:T(8,128)(2,1)S(1)} %bitcast.1373), kind=kOutput, calls=%fused_computation.150 | convolution fusion | flops 38733369344 | bytes 32556032 | tf_op jit(solution)/shard_map/transpose(jvp(bmk,bkn->bmn))/dot_general | solution.py:42
  1600.5 25.8 %fusion.85 = f32[4103,1536]{1,0:T(8,128)} fusion(bf16[1,4103,512]{2,1,0:T(8,128)(2,1)} %fusion.88, f32[8192,512]{1,0:T(8,128)} %subtract_add_fusion.4), kind=kOutput, calls=%fused_computation.141 | convolution fusion | flops 38720765952 | bytes 32557056 | tf_op jit(solution)/shard_map/transpose(jvp(bmk,bkn->bmn))/dot_general | solution.py:42
  1626.3 18.2 fusion.480
  1644.5 64.9 %pad.277 = f32[8207,512]{1,0:T(8,128)} pad(f32[4103,512]{1,0:T(8,128)} %get-tuple-element.201, f32[]{:T(128)} %constant.65.clone.1), padding=2_0_1x0_0_0 | pad | bytes 25210884 | tf_op jit(solution)/shard_map/transpose(jvp())/pad | solution.py:58
  1709.4 64.4 %pad.278 = f32[8207,512]{1,0:T(8,128)} pad(f32[4103,512]{1,0:T(8,128)} %get-tuple-element.199, f32[]{:T(128)} %constant.65.clone.1), padding=1_1_1x0_0_0 | pad | bytes 25210884 | tf_op jit(solution)/shard_map/transpose(jvp())/pad | solution.py:58
  1773.8 64.4 %pad.279 = f32[8207,512]{1,0:T(8,128)} pad(f32[4103,512]{1,0:T(8,128)} %get-tuple-element.200, f32[]{:T(128)} %constant.65.clone.1), padding=0_2_1x0_0_0 | pad | bytes 25210884 | tf_op jit(solution)/shard_map/transpose(jvp())/pad | solution.py:58
  1838.2 34.3 %fusion.55 = bf16[1,8207,512]{2,1,0:T(8,128)(2,1)} fusion(f32[8207,512]{1,0:T(8,128)} %get-tuple-element.195, f32[8207,512]{1,0:T(8,128)} %pad.279, f32[8207,512]{1,0:T(8,128)} %pad.277, f32[8207,512]{1,0:T(8,128)} %pad.278, f32[8207,512]{1,0:T(8,128)} %copy-done, bf16[1,8207,512]{2,1,0:T(8,128)(2,1)} %copy-done.2), kind=kLoop, calls=%fused_computation.94 | loop fusion | flops 79837696 | bytes 100847616 | tf_op jit(solution)/shard_map/transpose(jvp())/convert_element_type | solution.py:30
  1904.8 44.1 %all-reduce.72 = (f32[]{:T(128)}, f32[]{:T(128)}, f32[12,512]{1,0:T(8,128)S(1)}, f32[10,768]{1,0:T(8,128)S(1)}) all-reduce(f32[]{:T(128)S(6)} %div.229, f32[]{:T(128)S(6)} %add.751, f32[12,512]{1,0:T(8,128)S(1)} %pad_add_fusion.9, f32[10,768]{1,0:T(8,128)S(1)} %add_add_fusion.5), channel_id=1, replica_groups=mesh['dp'=8,'narrow'=4] {'dp','narrow'}, use_global_device_ids=true, to_apply=%region_22.23 | all-reduce | flops 13826 | bytes 110608 | tf_op jit(solution)/shard_map/psum | solution.py:334
  (940 shorter events, 876.4 us)
Async XLA Ops:
  7.2 26.5 %all-gather.21.cloned.1.call-start = ((), (), s32[]{:S(2)}) async-start(), calls=%async_computation.10 | async-start | bytes 2211840 | tf_op jit(solution)/shard_map/all_gather | solution.py:293
  9.3 65.5 %copy-start.135 = (f32[41040]{0:T(1024)S(1)}, f32[41040]{0:T(1024)}, u32[]{:S(2)}) copy-start(f32[41040]{0:T(1024)} %param.20) | copy-start | bytes 492484
  9.3 292.2 %all-gather.17.cloned.1.call-start = ((), (), s32[]{:S(2)}) async-start(), calls=%async_computation.8 | async-start | bytes 2211840 | tf_op jit(solution)/shard_map/all_gather | solution.py:292
  11.4 86.9 %copy-start.142 = (f32[12,512]{1,0:T(8,128)S(1)}, f32[12,512]{1,0:T(8,128)}, u32[]{:S(2)}) copy-start(f32[12,512]{1,0:T(8,128)} %param.24) | copy-start | bytes 73732
  11.4 290.2 %all-gather.15.cloned.1.call-start = ((), (), s32[]{:S(2)}) async-start(), calls=%async_computation.7 | async-start | bytes 3981312 | tf_op jit(solution)/shard_map/all_gather | solution.py:299
  22.3 315.0 %all-gather.13.cloned.1.call-start = ((), (), s32[]{:S(2)}) async-start(), calls=%async_computation.6 | async-start | bytes 8650752 | tf_op jit(solution)/shard_map/all_gather | solution.py:304
  23.1 744.5 %all-gather.23.cloned.1.call-start = ((), (), s32[]{:S(2)}) async-start(), calls=%async_computation.11 | async-start | bytes 15925248 | tf_op jit(solution)/shard_map/all_gather | solution.py:298
  33.7 803.3 %all-gather.19.cloned.1.call-start = ((), (), s32[]{:S(2)}) async-start(), calls=%async_computation.9 | async-start | bytes 15925248 | tf_op jit(solution)/shard_map/all_gather | solution.py:297
  114.5 40.5 %copy-start = (f32[8207,512]{1,0:T(8,128)}, f32[8207,512]{1,0:T(8,128)S(1)}, u32[]{:S(2)}) copy-start(f32[8207,512]{1,0:T(8,128)S(1)} %fusion.404) | copy-start | bytes 50423812
  115.7 39.3 %copy-start.2 = (bf16[1,8207,512]{2,1,0:T(8,128)(2,1)}, bf16[1,8207,512]{2,1,0:T(8,128)(2,1)S(1)}, u32[]{:S(2)}) copy-start(bf16[1,8207,512]{2,1,0:T(8,128)(2,1)S(1)} %convert_bitcast_fusion) | copy-start | bytes 25211908
  254.9 41.8 %copy-start.138 = (f32[10,768]{1,0:T(8,128)S(1)}, f32[10,768]{1,0:T(8,128)}, u32[]{:S(2)}) copy-start(f32[10,768]{1,0:T(8,128)} %param.27) | copy-start | bytes 92164
  254.9 41.8 %copy-start.220 = (s32[128]{0:T(128)S(1)}, s32[128]{0:T(128)}, u32[]{:S(2)}) copy-start(s32[128]{0:T(128)} %param.21) | copy-start | bytes 1540
  254.9 42.6 %copy-start.139 = (f32[10,768]{1,0:T(8,128)S(1)}, f32[10,768]{1,0:T(8,128)}, u32[]{:S(2)}) copy-start(f32[10,768]{1,0:T(8,128)} %param.30) | copy-start | bytes 92164
  301.6 1063.1 %reduce-scatter.11.cloned.1.call-start = ((), (), s32[]{:S(2)}) async-start(), calls=%async_computation.12 | async-start | bytes 10616832 | tf_op jit(solution)/shard_map/reduce_scatter | solution.py:323
  659.2 42.9 %copy-start.32 = (f32[128,768]{1,0:T(8,128)}, f32[128,768]{1,0:T(8,128)S(1)}, u32[]{:S(2)}) copy-start(f32[128,768]{1,0:T(8,128)S(1)} %get-tuple-element.175) | copy-start | bytes 1179652
  767.2 96.9 %copy-start.183 = (f32[128]{0:T(128)}, f32[128]{0:T(128)S(1)}, u32[]{:S(2)}) copy-start(f32[128]{0:T(128)S(1)} %broadcast_multiply_fusion.6) | copy-start | bytes 1540
  767.4 96.7 %copy-start.194 = (f32[128]{0:T(128)}, f32[128]{0:T(128)S(1)}, u32[]{:S(2)}) copy-start(f32[128]{0:T(128)S(1)} %fusion.431) | copy-start | bytes 1540
  767.6 96.5 %copy-start.92 = (bf16[128,768]{1,0:T(8,128)(2,1)}, bf16[128,768]{1,0:T(8,128)(2,1)S(1)}, u32[]{:S(2)}) copy-start(bf16[128,768]{1,0:T(8,128)(2,1)S(1)} %fusion.441) | copy-start | bytes 589828
  877.6 38.1 %slice-start = ((s8[28311552]{0:T(1024)(128)(4,1)}), s8[4194304]{0:T(1024)(128)(4,1)S(1)}, s32[]{:S(2)}) async-start(s8[28311552]{0:T(1024)(128)(4,1)} %bitcast.1349), calls=%async_computation.18 | async-start | bytes 8388608
  878.2 37.4 %slice-start.1 = ((s8[28311552]{0:T(1024)(128)(4,1)}), s8[4194304]{0:T(1024)(128)(4,1)S(1)}, s32[]{:S(2)}) async-start(s8[28311552]{0:T(1024)(128)(4,1)} %bitcast.1349), calls=%async_computation.19 | async-start | bytes 8388608
  1004.0 360.7 %reduce-scatter.13.cloned.1.call-start = ((), (), s32[]{:S(2)}) async-start(), calls=%async_computation.13 | async-start | bytes 10616832 | tf_op jit(solution)/shard_map/reduce_scatter | solution.py:323
  1004.8 495.9 %reduce-scatter.15.cloned.1.call-start = ((), (), s32[]{:S(2)}) async-start(), calls=%async_computation.14 | async-start | bytes 10616832 | tf_op jit(solution)/shard_map/reduce_scatter | solution.py:323
  1005.5 872.9 %reduce-scatter.21.cloned.1.call-start = ((), (), s32[]{:S(2)}) async-start(), calls=%async_computation.17 | async-start | bytes 7962624
  1084.8 814.3 %reduce-scatter.17.cloned.1.call-start = ((), (), s32[]{:S(2)}) async-start(), calls=%async_computation.15 | async-start | bytes 4423680 | tf_op jit(solution)/shard_map/reduce_scatter | solution.py:328
  1093.0 46.0 %copy-start.19 = (f32[512,512]{0,1:T(8,128)S(1)}, f32[512,512]{0,1:T(8,128)}, u32[]{:S(2)}) copy-start(f32[512,512]{0,1:T(8,128)} %copy-done.18) | copy-start | bytes 3145732
  1093.0 46.0 %copy-start.36 = (f32[512,512]{0,1:T(8,128)S(1)}, f32[512,512]{0,1:T(8,128)}, u32[]{:S(2)}) copy-start(f32[512,512]{0,1:T(8,128)} %copy-done.35) | copy-start | bytes 3145732
  1093.0 45.9 %copy-start.44 = (bf16[1,512,512]{1,2,0:T(8,128)(2,1)S(1)}, bf16[1,512,512]{1,2,0:T(8,128)(2,1)}, u32[]{:S(2)}) copy-start(bf16[1,512,512]{1,2,0:T(8,128)(2,1)} %copy-done.43) | copy-start | bytes 1572868
  1504.9 397.5 %reduce-scatter.19.cloned.1.call-start = ((), (), s32[]{:S(2)}) async-start(), calls=%async_computation.16 | async-start | bytes 17301504 | tf_op jit(solution)/shard_map/reduce_scatter | solution.py:333
  1838.2 34.3 %copy-start.49 = (f32[8207,10]{0,1:T(8,128)S(1)}, f32[8207,10]{0,1:T(8,128)}, u32[]{:S(2)}) copy-start(f32[8207,10]{0,1:T(8,128)} %copy-done.48) | copy-start | bytes 984844
  1878.4 73.8 %copy-start.130 = (f32[3,96,768]{2,1,0:T(8,128)S(1)}, f32[3,96,768]{2,1,0:T(8,128)}, u32[]{:S(2)}) copy-start(f32[3,96,768]{2,1,0:T(8,128)} %param.39) | copy-start | bytes 2654212
  1895.5 2.1 collective-permute-start
  1898.4 53.8 %copy-start.77 = (f32[96,596]{0,1:T(8,128)}, f32[96,596]{0,1:T(8,128)S(1)}, u32[]{:S(2)}) copy-start(f32[96,596]{0,1:T(8,128)S(1)} %concatenate.34) | copy-start | bytes 686596
  (236 other events, 1876.8 us)
Sparse Core Ops, SparseCore 0:
  10.2 23.4 all-gather.20
  35.8 20.9 all-gather.16
  59.5 65.1 all-gather.14
  128.0 76.0 all-gather.12
  206.2 194.1 all-gather.22
  402.5 193.7 all-gather.18
  1004.1 164.3 reduce-scatter.10
  1172.1 162.5 reduce-scatter.12
  1338.3 162.3 reduce-scatter.14
  1504.2 128.0 reduce-scatter.20
  1635.1 39.4 reduce-scatter.16
  1676.8 182.9 reduce-scatter.18
